TPU v7x, 256 devices: a whole 4x4x8 slice. The times are simulated.
256 devices in a mesh: dp: 32 (over x, z), mp: 8 (over y, core).
Axes of the slice: x: 4, y: 4, z: 8, core: 2. Of those that a mesh axis runs over, the one named last changes fastest.
Arguments:
- grad_parts: bfloat16 [32, 16, 1024, 1024], P('dp', None, None, 'mp'), may hold values from -6 to 6
- owners: int32 [16], replicated, may hold values from 0 to 7, as said below
- left_stat: float32 [32, 1024, 1024], P('mp', 'dp'), may hold values from -1 to 8
- right_stat: float32 [32, 1024, 1024], P('mp', 'dp'), may hold values from -1 to 8
- left_root: bfloat16 [32, 1024, 1024], P('mp', 'dp'), may hold values from -1 to 9
- right_root: bfloat16 [32, 1024, 1024], P('mp'), may hold values from -1 to 3
- first_moment: float32 [32, 1024, 1024], P('mp', 'dp'), may hold values from -32 to 32
- second_moment: float32 [32, 1024, 1024], P('mp', 'dp'), may hold values from 0.5 to 2
- vec_grad: bfloat16 [32, 73728], P('dp', 'mp'), may hold values from -3 to 3
- vec_first: float32 [73728], P('mp'), may hold values from -4 to 4
- vec_second: float32 [73728], P('mp'), may hold values from 0.5 to 2
Outputs:
- block_update: bfloat16 [16, 1024, 1024], P(None, 'dp', 'mp')
- left_new: float32 [32, 1024, 1024], P('mp', 'dp')
- right_new: float32 [32, 1024, 1024], P('mp', 'dp')
- first_new: float32 [32, 1024, 1024], P('mp', 'dp')
- second_new: float32 [32, 1024, 1024], P('mp', 'dp')
- vec_update: bfloat16 [73728], P('mp')
- vec_first_new: float32 [73728], P('mp')
- vec_second_new: float32 [73728], P('mp')
Inputs may be any that keep to these rules, and one draw needn't show every extreme that they name: `owners`: no owner holds more than 4 blocks, and in every draw some owner holds exactly 4.
All inputs are finite; a program needn't handle non-finite values.
Results may differ from a plain program's by a relative error of at most 0.018.
Values may be sent and summed in bfloat16 or wider, within the bound.
A program may use at most 128 MiB of HBM per device.

v0:
```python
import jax
import jax.numpy as jnp
from jax import lax
from jax.sharding import PartitionSpec as P

beta_one = 0.9
beta_two = 0.95
adam_eps = 1e-08
graft_eps = 1e-06


def owner_table(owners, owner_count, slot_count):
    block_count = owners.shape[0]
    same = owners[:, None] == owners[None, :]
    earlier = lax.broadcasted_iota(jnp.int32, (block_count, block_count), 1) < lax.broadcasted_iota(
        jnp.int32, (block_count, block_count), 0
    )
    slots = jnp.sum((same & earlier).astype(jnp.int32), axis=1)
    owner_ids = lax.broadcasted_iota(jnp.int32, (owner_count, slot_count, block_count), 0)
    slot_ids = lax.broadcasted_iota(jnp.int32, (owner_count, slot_count, block_count), 1)
    return ((owners[None, None, :] == owner_ids) & (slots[None, None, :] == slot_ids)).astype(
        jnp.float32
    )


def body(
    grad_parts,
    owners,
    left_stat,
    right_stat,
    left_root,
    right_root,
    first_moment,
    second_moment,
    vec_grad,
    vec_first,
    vec_second,
):
    owner_count = lax.axis_size("mp")
    slot_count, row_count, order = left_stat.shape
    col_count = order // owner_count
    my_rows = lax.axis_index("dp") * row_count
    my_owner = lax.axis_index("mp")
    row_pieces = lax.psum_scatter(
        grad_parts[0].astype(jnp.float32).astype(jnp.bfloat16),
        "dp",
        scatter_dimension=1,
        tiled=True,
    ).astype(jnp.float32)
    selector = owner_table(owners, owner_count, slot_count)
    outgoing = jnp.einsum("ocb,brw->crow", selector, row_pieces, precision=lax.Precision.HIGHEST)
    incoming = lax.all_to_all(
        outgoing.astype(jnp.bfloat16), "mp", split_axis=2, concat_axis=2, tiled=True
    ).astype(outgoing.dtype)
    grad_rows = incoming.reshape(slot_count, row_count, order)
    mine = lax.dynamic_index_in_dim(selector, my_owner, 0, keepdims=False)
    used_mask = (jnp.sum(mine, axis=1) > 0.5)[:, None, None]
    rounded_rows = grad_rows.astype(jnp.bfloat16)
    shard_rows = lax.all_gather(rounded_rows, "dp", axis=1, tiled=True)
    left_part = jnp.einsum(
        "crk,cnk->crn", rounded_rows, shard_rows, preferred_element_type=jnp.float32
    )
    own_cols = lax.dynamic_slice_in_dim(shard_rows, my_rows, row_count, 2)
    right_acc = jnp.einsum("cnr,cnk->crk", own_cols, shard_rows, preferred_element_type=jnp.float32)
    applied_acc = jnp.einsum(
        "crn,cnk->crk", left_root, shard_rows, preferred_element_type=jnp.float32
    )
    scale = 1.0 / order
    left_new = jnp.where(used_mask, left_stat + left_part * scale, left_stat)
    right_new = jnp.where(used_mask, right_stat + right_acc * scale, right_stat)
    first_new = jnp.where(
        used_mask, beta_one * first_moment + (1.0 - beta_one) * grad_rows, first_moment
    )
    second_new = jnp.where(
        used_mask,
        beta_two * second_moment + (1.0 - beta_two) * grad_rows * grad_rows,
        second_moment,
    )
    adam = first_new / (jnp.sqrt(second_new) + adam_eps)
    precond = jnp.einsum(
        "crk,ckm->crm",
        applied_acc.astype(jnp.bfloat16),
        right_root,
        preferred_element_type=jnp.float32,
    )
    square_adam = jnp.sum(adam * adam, axis=(1, 2))
    square_pre = jnp.sum(precond * precond, axis=(1, 2))
    vec_local = vec_grad[0].astype(jnp.float32)
    square_adam, square_pre, vec_sum = lax.psum((square_adam, square_pre, vec_local), "dp")
    cells = float(order * order)
    graft = jnp.sqrt(square_adam / cells) / jnp.sqrt(square_pre / cells + graft_eps)
    update_rows = (precond * graft[:, None, None]).astype(jnp.bfloat16)
    returned = lax.all_to_all(
        update_rows.reshape(slot_count, row_count, owner_count, col_count),
        "mp",
        split_axis=2,
        concat_axis=2,
        tiled=True,
    )
    block_update = jnp.einsum(
        "ocb,crow->brw", selector.astype(jnp.bfloat16), returned, preferred_element_type=jnp.float32
    ).astype(jnp.bfloat16)
    vec_first_new = beta_one * vec_first + (1.0 - beta_one) * vec_sum
    vec_second_new = beta_two * vec_second + (1.0 - beta_two) * vec_sum * vec_sum
    vec_update = (vec_first_new / (jnp.sqrt(vec_second_new) + adam_eps)).astype(jnp.bfloat16)
    return (
        block_update,
        left_new,
        right_new,
        first_new,
        second_new,
        vec_update,
        vec_first_new,
        vec_second_new,
    )


def solution(mesh):
    placed = (
        P("dp", None, None, "mp"),
        P(),
        P("mp", "dp", None),
        P("mp", "dp", None),
        P("mp", "dp", None),
        P("mp", None, None),
        P("mp", "dp", None),
        P("mp", "dp", None),
        P("dp", "mp"),
        P("mp"),
        P("mp"),
    )
    return jax.shard_map(
        body,
        mesh=mesh,
        in_specs=placed,
        out_specs=(
            P(None, "dp", "mp"),
            P("mp", "dp", None),
            P("mp", "dp", None),
            P("mp", "dp", None),
            P("mp", "dp", None),
            P("mp"),
            P("mp"),
            P("mp"),
        ),
        check_vma=False,
    )
```

profile of v0, /device:TPU:1, one launch (start us, length us, event | category | flops | bytes accessed | tf_op | source)
XLA Modules:
  0.0 519.0 jit_solution(16055392310687253301)
XLA Ops:
  7.2 0.0 copy-start
  7.2 0.0 reduce-scatter.2.cloned.1.call-start
  7.2 0.7 reduce-scatter.2.cloned.1.call-update
  7.9 0.0 all-gather.2.cloned.1.call-start
  8.0 0.9 convert_reduce_fusion
  8.9 224.1 %reduce-scatter.2.cloned.1.call-done = bf16[16,32,128]{2,1,0:T(8,128)(2,1)} async-done(((bf16[16,1024,128]{2,1,0:T(8,128)(2,1)}), bf16[16,32,128]{2,1,0:T(8,128)(2,1)}) %reduce-scatter.2.cloned.1.call-update) | async-done | bytes 131088 | tf_op jit(solution)/shard_map/reduce_scatter | solution.py:44
  233.0 1.1 fusion.4
  234.2 16.5 %all_to_all.10 = bf16[4,32,8,128]{3,1,0,2:T(8,128)(2,1)S(1)} all-to-all(bf16[4,32,8,128]{3,1,0,2:T(8,128)(2,1)S(1)} %copy.31), channel_id=1, replica_groups=mesh['dp'=32,'mp'=8] {'mp'}, dimensions={2} | all-to-all | bytes 524288 | tf_op jit(solution)/shard_map/all_to_all | solution.py:52
  250.7 0.7 copy_bitcast_fusion
  251.4 0.0 all-gather.2.cloned.1.call-update
  251.4 0.8 convert_element_type.50
  252.2 0.7 fusion.19
  252.9 0.1 dynamic-slice_reduce_fusion
  253.0 2.6 multiply_reduce_fusion.1
  255.6 0.0 copy-start.2
  255.6 90.5 %all-gather.2.cloned.1.call-done = bf16[4,1024,1024]{2,1,0:T(8,128)(2,1)} async-done(((bf16[4,32,1024]{2,1,0:T(8,128)(2,1)}), bf16[4,1024,1024]{2,1,0:T(8,128)(2,1)}) %all-gather.2.cloned.1.call-update) | async-done | bytes 8388624 | tf_op jit(solution)/shard_map/all_gather | solution.py:59
  346.1 0.0 copy-done
  346.1 8.9 %multiply_reduce_fusion = (f32[4]{0:T(128)S(1)}, f32[4,32,1024]{2,1,0:T(8,128)S(1)}) fusion(bf16[4,1024,1024]{2,1,0:T(8,128)(2,1)} %param.16, bf16[4,32,1024]{2,1,0:T(8,128)(2,1)S(1)} %copy-done, bf16[4,1024,1024]{2,1,0:T(8,128)(2,1)} %all-gather.2.cloned.1.call-done), kind=kOutput, calls=%fused_computation.20 | convolution fusion | flops 537264128 | bytes 17563664 | tf_op jit(solution)/shard_map/crk,ckm->crm/dot_general | solution.py:80
  355.0 0.0 copy-start.3
  355.0 112.0 %all-reduce = (f32[4]{0:T(128)S(1)}, f32[4]{0:T(128)S(1)}, f32[9216]{0:T(1024)S(1)}) all-reduce(f32[4]{0:T(128)S(1)} %get-tuple-element.41, f32[4]{0:T(128)S(1)} %get-tuple-element.38, f32[9216]{0:T(1024)S(1)} %bitcast.49), channel_id=1, replica_groups=mesh['dp'=32,'mp'=8] {'dp'}, use_global_device_ids=true, to_apply=%region_6.7 | all-reduce | flops 9224 | bytes 73792 | tf_op jit(solution)/shard_map/psum | solution.py:89
  467.0 0.1 multiply_convert_fusion
  467.2 0.9 copy.33
  468.1 32.8 %all-to-all-start.1 = ((bf16[4,32,8,128]{3,0,1,2:T(4,128)(2,1)}), bf16[4,32,8,128]{3,0,1,2:T(4,128)(2,1)S(1)}, u32[]{:S(2)}, u32[]{:S(2)}) async-start(bf16[4,32,8,128]{3,0,1,2:T(4,128)(2,1)} %copy.33), calls=%async_computation.2 | async-start | bytes 524288 | tf_op jit(solution)/shard_map/all_to_all | solution.py:93
  500.9 0.0 copy-done.2
  500.9 0.0 copy-start.1
  500.9 0.0 copy-start.4
  500.9 0.0 copy-start.5
  500.9 0.0 copy-start.6
  501.0 6.9 %fusion.1 = f32[4,32,1024]{2,1,0:T(8,128)} fusion(f32[4,32,1024]{2,1,0:T(8,128)S(1)} %copy-done.2, bf16[4,1024,1024]{2,1,0:T(8,128)(2,1)} %all-gather.2.cloned.1.call-done, pred[4]{0:T(512)(128)(4,1)S(1)} %broadcast_compare_fusion, bf16[4,32,8,128]{3,1,0,2:T(8,128)(2,1)S(1)} %all_to_all.10), kind=kOutput, calls=%fused_computation.3 | convolution fusion | flops 268828672 | bytes 9699332 | tf_op jit(solution)/shard_map/crk,cnk->crn/dot_general | solution.py:60
  507.9 0.0 copy-done.3
  507.9 0.0 copy-done.1
  507.9 2.6 fusion.3
  510.5 0.0 copy-done.4
  510.5 0.0 copy-done.5
  510.5 0.6 divide_convert_fusion
  511.2 0.0 all-to-all-done.1
  511.2 0.0 copy-done.6
  511.2 0.3 fusion.5
  511.4 0.7 copy.36
  (4 shorter events, 0.1 us)
Async XLA Ops:
  7.2 338.9 %copy-start = (bf16[4,32,1024]{2,1,0:T(8,128)(2,1)S(1)}, bf16[4,32,1024]{2,1,0:T(8,128)(2,1)}, u32[]{:S(2)}) copy-start(bf16[4,32,1024]{2,1,0:T(8,128)(2,1)} %param.15) | copy-start | bytes 786436
  7.2 225.8 %reduce-scatter.2.cloned.1.call-start = ((), (), s32[]{:S(2)}) async-start(), calls=%async_computation.3 | async-start | bytes 4325376 | tf_op jit(solution)/shard_map/reduce_scatter | solution.py:44
  7.9 338.2 %all-gather.2.cloned.1.call-start = ((), (), s32[]{:S(2)}) async-start(), calls=%async_computation.4 | async-start | bytes 8650752 | tf_op jit(solution)/shard_map/all_gather | solution.py:59
  255.6 245.3 %copy-start.2 = (f32[4,32,1024]{2,1,0:T(8,128)S(1)}, f32[4,32,1024]{2,1,0:T(8,128)}, u32[]{:S(2)}) copy-start(f32[4,32,1024]{2,1,0:T(8,128)} %param.13) | copy-start | bytes 1572868
  355.0 152.9 %copy-start.3 = (f32[4,32,1024]{2,1,0:T(8,128)S(1)}, f32[4,32,1024]{2,1,0:T(8,128)}, u32[]{:S(2)}) copy-start(f32[4,32,1024]{2,1,0:T(8,128)} %param.14) | copy-start | bytes 1572868
  468.1 43.1 %all-to-all-start.1 = ((bf16[4,32,8,128]{3,0,1,2:T(4,128)(2,1)}), bf16[4,32,8,128]{3,0,1,2:T(4,128)(2,1)S(1)}, u32[]{:S(2)}, u32[]{:S(2)}) async-start(bf16[4,32,8,128]{3,0,1,2:T(4,128)(2,1)} %copy.33), calls=%async_computation.2 | async-start | bytes 524288 | tf_op jit(solution)/shard_map/all_to_all | solution.py:93
  500.9 7.0 %copy-start.1 = (bf16[4,1024,1024]{2,1,0:T(8,128)(2,1)S(1)}, bf16[4,1024,1024]{2,1,0:T(8,128)(2,1)}, u32[]{:S(2)}) copy-start(bf16[4,1024,1024]{2,1,0:T(8,128)(2,1)} %all-gather.2.cloned.1.call-done) | copy-start | bytes 25165828
  500.9 9.6 %copy-start.4 = (f32[9216]{0:T(1024)S(1)}, f32[9216]{0:T(1024)}, u32[]{:S(2)}) copy-start(f32[9216]{0:T(1024)} %param.21) | copy-start | bytes 110596
  500.9 9.6 %copy-start.5 = (f32[9216]{0:T(1024)S(1)}, f32[9216]{0:T(1024)}, u32[]{:S(2)}) copy-start(f32[9216]{0:T(1024)} %param.20) | copy-start | bytes 110596
  500.9 10.2 %copy-start.6 = (s32[16]{0:T(128)S(1)}, s32[16]{0:T(128)}, u32[]{:S(2)}) copy-start(s32[16]{0:T(128)} %param.12) | copy-start | bytes 196
Sparse Core Ops, SparseCore 0:
  11.9 221.0 reduce-scatter.1
  251.5 94.4 all-gather.1
where the time goes:
time: 519 us
  waiting for transfers between devices  315 us (61%)
  blocking collectives  129 us (25%)
  starting transfers between devices  32.9 us (6%)
  matrix products  19.8 us (4%)
  between operations  14.1 us (3%)
  other arithmetic  5.83 us (1%)
    reduce_scatter x1, waiting for transfers between devices, body(): lax.psum_scatter(grad_parts[0].astype(jnp.float32).astype(jnp.bfloat16),...  224 us
    psum x1, blocking collectives, body(): lax.psum((square_adam, square_pre, vec_local), 'dp')  112 us
    all_gather x1, waiting for transfers between devices, body(): shard_rows = lax.all_gather(rounded_rows, 'dp', axis=1, tiled=True)  90.5 us
    all_to_all x1, starting transfers between devices, body(): lax.all_to_all(update_rows.reshape(slot_count, row_count, owner_count, co...  32.8 us
    all_to_all x1, blocking collectives, body(): lax.all_to_all(outgoing.astype(jnp.bfloat16), 'mp', split_axis=2, concat_...  16.5 us
  transfers between devices with their start and end apart: 3, of which 2 were waited for; matrix products, arithmetic and copies ran while one was open for 3% of the time, Pallas kernels for 0%

commit v1 on v0

--- a/solution.py
+++ b/solution.py
@@ -85,8 +85,10 @@
     )
     square_adam = jnp.sum(adam * adam, axis=(1, 2))
     square_pre = jnp.sum(precond * precond, axis=(1, 2))
-    vec_local = vec_grad[0].astype(jnp.float32)
-    square_adam, square_pre, vec_sum = lax.psum((square_adam, square_pre, vec_local), "dp")
+    squares = lax.all_gather(jnp.stack([square_adam, square_pre]), "dp")
+    square_adam, square_pre = jnp.sum(squares, axis=0)
+    vec_all = lax.all_gather(vec_grad[0], "dp")
+    vec_sum = jnp.sum(vec_all.astype(jnp.float32), axis=0)
     cells = float(order * order)
     graft = jnp.sqrt(square_adam / cells) / jnp.sqrt(square_pre / cells + graft_eps)
     update_rows = (precond * graft[:, None, None]).astype(jnp.bfloat16)

time: 519 us -> 421 us (0.81)
  blocking collectives: 129 us -> 87.3 us
  waiting for transfers between devices: 315 us -> 276 us
  starting transfers between devices: 32.9 us -> 15.5 us
    psum x1 -> x0, blocking collectives: 112 us -> none  [body(): lax.psum((square_adam, square_pre, vec_local), 'dp')]
    all_gather x0 -> x2, blocking collectives: none -> 70.8 us  [the longest x1 39.8 us: body(): vec_all = lax.all_gather(vec_grad[0], 'dp')]
    all_gather x1, waiting for transfers between devices: 90.5 us -> 51.2 us  [body(): shard_rows = lax.all_gather(rounded_rows, 'dp', axis=1, tiled=True)]
    all_to_all x1, starting transfers between devices: 32.8 us -> 15.5 us  [body(): lax.all_to_all(update_rows.reshape(slot_count, row_count, owner_count, co...]
where the time goes in v1:
time: 421 us; the launch traced here: 420 us
  waiting for transfers between devices  276 us (66%)
  blocking collectives  87.3 us (21%)
  matrix products  19.8 us (5%)
  starting transfers between devices  15.5 us (4%)
  between operations  14.2 us (3%)
  other arithmetic  5.23 us (1%)
    reduce_scatter x1, waiting for transfers between devices, body(): lax.psum_scatter(grad_parts[0].astype(jnp.float32).astype(jnp.bfloat16),...  224 us
    all_gather x1, waiting for transfers between devices, body(): shard_rows = lax.all_gather(rounded_rows, 'dp', axis=1, tiled=True)  51.2 us
    all_gather x1, blocking collectives, body(): vec_all = lax.all_gather(vec_grad[0], 'dp')  39.8 us
    all_gather x1, blocking collectives, body(): squares = lax.all_gather(jnp.stack([square_adam, square_pre]), 'dp')  31 us
    all_to_all x1, blocking collectives, body(): lax.all_to_all(outgoing.astype(jnp.bfloat16), 'mp', split_axis=2, concat_...  16.5 us
    all_to_all x1, starting transfers between devices, body(): lax.all_to_all(update_rows.reshape(slot_count, row_count, owner_count, co...  15.5 us
    dot_general x1, matrix products, body(): jnp.einsum('crk,ckm->crm', applied_acc.astype(jnp.bfloat16), right_root,...  8.86 us
  transfers between devices with their start and end apart: 3, of which 2 were waited for; matrix products, arithmetic and copies ran while one was open for 3% of the time, Pallas kernels for 0%

profile of v1, /device:TPU:1, one launch (start us, length us, event | category | flops | bytes accessed | tf_op | source)
XLA Modules:
  0.0 420.2 jit_solution(11740701285527777204)
XLA Ops:
  7.2 0.0 copy-start
  7.2 0.0 copy-start.6
  7.2 0.0 copy-start.7
  7.2 0.0 copy-start.3
  7.2 0.0 copy-start.4
  7.2 0.0 reduce-scatter.2.cloned.1.call-start
  7.3 0.7 reduce-scatter.2.cloned.1.call-update
  8.0 0.0 all-gather.5.cloned.1.call-start
  8.0 0.9 convert_reduce_fusion.1
  8.9 223.8 %reduce-scatter.2.cloned.1.call-done = bf16[16,32,128]{2,1,0:T(8,128)(2,1)} async-done(((bf16[16,1024,128]{2,1,0:T(8,128)(2,1)}), bf16[16,32,128]{2,1,0:T(8,128)(2,1)}) %reduce-scatter.2.cloned.1.call-update) | async-done | bytes 131088 | tf_op jit(solution)/shard_map/reduce_scatter | solution.py:44
  232.8 1.1 fusion.4
  233.9 16.5 %all_to_all.10 = bf16[4,32,8,128]{3,1,0,2:T(8,128)(2,1)S(1)} all-to-all(bf16[4,32,8,128]{3,1,0,2:T(8,128)(2,1)S(1)} %copy.31), channel_id=1, replica_groups=mesh['dp'=32,'mp'=8] {'mp'}, dimensions={2} | all-to-all | bytes 524288 | tf_op jit(solution)/shard_map/all_to_all | solution.py:52
  250.4 0.7 copy_bitcast_fusion
  251.2 0.0 all-gather.5.cloned.1.call-update
  251.2 0.7 fusion.19
  251.9 0.1 dynamic-slice_reduce_fusion
  252.0 39.8 %all-gather.2 = bf16[32,1,9216]{2,1,0:T(2,128)(2,1)S(1)} all-gather(bf16[1,1,9216]{2,1,0:T(2,128)(2,1)} %bitcast.55), channel_id=1, replica_groups=mesh['dp'=32,'mp'=8] {'dp'}, dimensions={0}, use_global_device_ids=true | all-gather | bytes 608256 | tf_op jit(solution)/shard_map/all_gather | solution.py:90
  291.8 1.3 convert_reduce_fusion
  293.1 0.0 copy-done.6
  293.1 0.0 copy-done.7
  293.1 0.6 divide_convert_fusion
  293.8 0.0 copy-done.3
  293.8 0.0 copy-done.4
  293.8 1.4 multiply_reduce_fusion.1
  295.2 0.0 copy-start.2
  295.2 51.2 %all-gather.5.cloned.1.call-done = bf16[4,1024,1024]{2,1,0:T(8,128)(2,1)} async-done(((bf16[4,32,1024]{2,1,0:T(8,128)(2,1)}), bf16[4,1024,1024]{2,1,0:T(8,128)(2,1)}) %all-gather.5.cloned.1.call-update) | async-done | bytes 8388624 | tf_op jit(solution)/shard_map/all_gather | solution.py:59
  346.4 0.0 copy-done
  346.4 8.9 %multiply_reduce_fusion = (f32[4]{0:T(128)S(1)}, f32[4,32,1024]{2,1,0:T(8,128)S(1)}) fusion(bf16[4,1024,1024]{2,1,0:T(8,128)(2,1)} %param.16, bf16[4,32,1024]{2,1,0:T(8,128)(2,1)S(1)} %copy-done, bf16[4,1024,1024]{2,1,0:T(8,128)(2,1)} %all-gather.5.cloned.1.call-done), kind=kOutput, calls=%fused_computation.21 | convolution fusion | flops 537264128 | bytes 17563664 | tf_op jit(solution)/shard_map/crk,ckm->crm/dot_general | solution.py:80
  355.2 0.0 copy-start.5
  355.2 31.0 %all-gather.1 = f32[32,2,4]{2,1,0:T(2,128)S(1)} all-gather(f32[1,2,4]{2,1,0:T(2,128)S(1)} %maximum_bitcast_fusion), channel_id=2, replica_groups=mesh['dp'=32,'mp'=8] {'dp'}, dimensions={0}, use_global_device_ids=true | all-gather | bytes 1056 | tf_op jit(solution)/shard_map/all_gather | solution.py:88
  386.3 0.1 multiply_convert_fusion
  386.5 0.9 copy.33
  387.4 15.5 %all-to-all-start.1 = ((bf16[4,32,8,128]{3,0,1,2:T(4,128)(2,1)}), bf16[4,32,8,128]{3,0,1,2:T(4,128)(2,1)S(1)}, u32[]{:S(2)}, u32[]{:S(2)}) async-start(bf16[4,32,8,128]{3,0,1,2:T(4,128)(2,1)} %copy.33), calls=%async_computation.2 | async-start | bytes 524288 | tf_op jit(solution)/shard_map/all_to_all | solution.py:95
  402.8 0.0 copy-done.2
  402.9 0.0 copy-start.1
  402.9 0.0 copy-start.8
  402.9 6.9 %fusion.1 = f32[4,32,1024]{2,1,0:T(8,128)} fusion(f32[4,32,1024]{2,1,0:T(8,128)S(1)} %copy-done.2, bf16[4,1024,1024]{2,1,0:T(8,128)(2,1)} %all-gather.5.cloned.1.call-done, pred[4]{0:T(512)(128)(4,1)S(1)} %broadcast_compare_fusion, bf16[4,32,8,128]{3,1,0,2:T(8,128)(2,1)S(1)} %all_to_all.10), kind=kOutput, calls=%fused_computation.3 | convolution fusion | flops 268828672 | bytes 9699332 | tf_op jit(solution)/shard_map/crk,cnk->crn/dot_general | solution.py:60
  409.8 0.0 copy-done.5
  409.8 0.0 copy-done.1
  409.8 2.6 fusion.3
  412.4 0.0 all-to-all-done.1
  412.4 0.0 copy-done.8
  412.4 0.3 fusion.5
  412.7 0.7 copy.36
  (6 shorter events, 0.2 us)
Async XLA Ops:
  7.2 339.2 %copy-start = (bf16[4,32,1024]{2,1,0:T(8,128)(2,1)S(1)}, bf16[4,32,1024]{2,1,0:T(8,128)(2,1)}, u32[]{:S(2)}) copy-start(bf16[4,32,1024]{2,1,0:T(8,128)(2,1)} %param.15) | copy-start | bytes 786436
  7.2 285.9 %copy-start.6 = (f32[9216]{0:T(1024)S(1)}, f32[9216]{0:T(1024)}, u32[]{:S(2)}) copy-start(f32[9216]{0:T(1024)} %param.21) | copy-start | bytes 110596
  7.2 285.9 %copy-start.7 = (f32[9216]{0:T(1024)S(1)}, f32[9216]{0:T(1024)}, u32[]{:S(2)}) copy-start(f32[9216]{0:T(1024)} %param.20) | copy-start | bytes 110596
  7.2 286.6 %copy-start.3 = (f32[4,32,1024]{2,1,0:T(8,128)S(1)}, f32[4,32,1024]{2,1,0:T(8,128)}, u32[]{:S(2)}) copy-start(f32[4,32,1024]{2,1,0:T(8,128)} %param.18) | copy-start | bytes 1572868
  7.2 286.6 %copy-start.4 = (f32[4,32,1024]{2,1,0:T(8,128)S(1)}, f32[4,32,1024]{2,1,0:T(8,128)}, u32[]{:S(2)}) copy-start(f32[4,32,1024]{2,1,0:T(8,128)} %param.17) | copy-start | bytes 1572868
  7.2 225.5 %reduce-scatter.2.cloned.1.call-start = ((), (), s32[]{:S(2)}) async-start(), calls=%async_computation.3 | async-start | bytes 4325376 | tf_op jit(solution)/shard_map/reduce_scatter | solution.py:44
  8.0 338.4 %all-gather.5.cloned.1.call-start = ((), (), s32[]{:S(2)}) async-start(), calls=%async_computation.4 | async-start | bytes 8650752 | tf_op jit(solution)/shard_map/all_gather | solution.py:59
  295.2 107.7 %copy-start.2 = (f32[4,32,1024]{2,1,0:T(8,128)S(1)}, f32[4,32,1024]{2,1,0:T(8,128)}, u32[]{:S(2)}) copy-start(f32[4,32,1024]{2,1,0:T(8,128)} %param.13) | copy-start | bytes 1572868
  355.2 54.6 %copy-start.5 = (f32[4,32,1024]{2,1,0:T(8,128)S(1)}, f32[4,32,1024]{2,1,0:T(8,128)}, u32[]{:S(2)}) copy-start(f32[4,32,1024]{2,1,0:T(8,128)} %param.14) | copy-start | bytes 1572868
  387.4 25.0 %all-to-all-start.1 = ((bf16[4,32,8,128]{3,0,1,2:T(4,128)(2,1)}), bf16[4,32,8,128]{3,0,1,2:T(4,128)(2,1)S(1)}, u32[]{:S(2)}, u32[]{:S(2)}) async-start(bf16[4,32,8,128]{3,0,1,2:T(4,128)(2,1)} %copy.33), calls=%async_computation.2 | async-start | bytes 524288 | tf_op jit(solution)/shard_map/all_to_all | solution.py:95
  402.9 6.9 %copy-start.1 = (bf16[4,1024,1024]{2,1,0:T(8,128)(2,1)S(1)}, bf16[4,1024,1024]{2,1,0:T(8,128)(2,1)}, u32[]{:S(2)}) copy-start(bf16[4,1024,1024]{2,1,0:T(8,128)(2,1)} %all-gather.5.cloned.1.call-done) | copy-start | bytes 25165828
  402.9 9.6 %copy-start.8 = (s32[16]{0:T(128)S(1)}, s32[16]{0:T(128)}, u32[]{:S(2)}) copy-start(s32[16]{0:T(128)} %param.12) | copy-start | bytes 196
Sparse Core Ops, SparseCore 0:
  12.0 220.7 reduce-scatter.1
  251.3 94.9 all-gather.4

commit v2 on v0

v2 whole, which is shorter than its diff:
```python
import heapq

import jax
import jax.numpy as jnp
from jax import lax
from jax.experimental import pallas as pl
from jax.experimental.pallas import tpu as pltpu
from jax.sharding import PartitionSpec as P

beta_one = 0.9
beta_two = 0.95
adam_eps = 1e-08
graft_eps = 1e-06

MESH = pl.DeviceIdType.MESH
NX, NZ, NY, NC = 4, 8, 4, 2
N_MP = NY * NC
BLOCKS, SLOT_COUNT, ROWS, ORDER, COLS = 16, 4, 32, 1024, 128
HALF = ROWS // NC
N_SEMS = 224
bf16, f32 = jnp.bfloat16, jnp.float32


def kernel(
    owners, grad, lroot, rroot, lstat, rstat, mom1, mom2, vecg,
    upd_out, left_out, right_out, first_out, second_out, vec_out,
    gin, rbz1, rbz2, ra1, rr1, rs1, ra2, rr2, rs2, r1, r2, fin, gfull,
    ly, lsel, lhome, lhs1, lhs2, res, held0, held1, held2, held3, stage, won, rrv, lsv, rsv, m1v, m2v,
    out_l, out_r, out_1, out_2, prec, upd_in, norm_me, norm_z, norm_x, norm_m, vx, vs, vz, upd_s,
    send_sems, recv_sems, local_sems,
):
    dp, mp = lax.axis_index("dp"), lax.axis_index("mp")
    x, z = dp // NZ, lax.rem(dp, NZ)
    y, c = mp // NC, lax.rem(mp, NC)
    held = (held0, held1, held2, held3)
    counts = {"remote": 0, "local": 0}
    sent = []

    def xdev(k):
        return (lax.rem(x + k + NX, NX) * NZ + z, mp)

    def zdev(k):
        return (x * NZ + lax.rem(z + k + NZ, NZ), mp)

    def ydev(k):
        return (dp, lax.rem(y + k + NY, NY) * NC + c)

    sibling = (dp, y * NC + 1 - c)

    def send(src, dst, device):
        i = counts["remote"]
        counts["remote"] += 1
        copy = pltpu.make_async_remote_copy(
            src_ref=src, dst_ref=dst, send_sem=send_sems.at[i], recv_sem=recv_sems.at[i],
            device_id=device, device_id_type=MESH,
        )
        copy.start()
        sent.append(copy)
        return copy

    def local(src, dst):
        i = counts["local"]
        counts["local"] += 1
        copy = pltpu.make_async_copy(src, dst, local_sems.at[i])
        copy.start()
        return copy

    load_z = local(grad.at[:, 2:4], gin.at[:, 2:4])
    load_x = local(grad.at[:, 0:2], gin.at[:, 0:2])
    load_l = local(lroot.at[:, c], ly.at[y, c])

    barrier = pltpu.get_barrier_semaphore()
    partners = [xdev(k) for k in range(1, NX)] + [zdev(k) for k in range(1, NZ)]
    partners += [(dp, lax.rem(mp + k, N_MP)) for k in range(1, N_MP)]
    for device in partners:
        pl.semaphore_signal(barrier, inc=1, device_id=device, device_id_type=MESH)

    load_r = local(rroot, rrv)
    load_1 = local(mom1, m1v)
    load_2 = local(mom2, m2v)
    load_ls = local(lstat, lsv)
    load_rs = local(rstat, rsv)

    own = [owners[b] for b in range(BLOCKS)]
    slot = []
    for b in range(BLOCKS):
        s = 0
        for a in range(b):
            s = s + jnp.where(own[a] == own[b], 1, 0)
        slot.append(s)
    place = [0] + [jnp.minimum(s, SLOT_COUNT - 1) for s in slot[1:]]

    def picks(who):
        chosen = []
        for s in range(SLOT_COUNT):
            p = jnp.int32(0)
            for b in range(BLOCKS):
                p = p + jnp.where((own[b] == who) & (slot[b] == s), b, 0)
            chosen.append(p)
        return chosen

    mine, theirs = picks(mp), picks(y * NC + 1 - c)
    owned = jnp.int32(0)
    for b in range(BLOCKS):
        owned = owned + jnp.where(own[b] == mp, 1, 0)

    load_z.wait()
    load_x.wait()
    pl.semaphore_wait(barrier, len(partners))

    def accumulate(into, term):
        into[...] = into[...] + term[...]

    queue = []
    clock = {"t": 0.0, "n": 0}
    done = set()

    def spawn(gen, t):
        clock["n"] += 1
        heapq.heappush(queue, (t, clock["n"], gen))

    def run():
        while queue:
            t, _, gen = heapq.heappop(queue)
            clock["t"] = t
            try:
                nxt = next(gen)
            except StopIteration:
                continue
            spawn(gen, nxt)

    def need(*names):
        while not all(n in done for n in names):
            yield clock["t"] + 0.25

    def z_stream(name, d, h, term, rb, t0, dt):
        steps = 4 if (h == 0) == (d == 1) else 3
        di = 0 if d == 1 else 1
        copy = send(term(lax.rem(z + d * steps + NZ, NZ), h), rb.at[di, h, 0], zdev(d))
        for s in range(steps):
            yield t0 + (s + 1) * dt
            copy.wait_recv()
            if s < steps - 1:
                accumulate(rb.at[di, h, s], term(lax.rem(z + d * (steps - 1 - s) + NZ, NZ), h))
                copy = send(rb.at[di, h, s], rb.at[di, h, s + 1], zdev(d))
        done.add((name, d, h))

    def last(d, h):
        return 3 if (h == 0) == (d == 1) else 2

    def x_stream(name, term, ra, rr, rs, put, times):
        first, raw, second = {}, {}, {}
        for d, di in ((1, 0), (-1, 1)):
            first[d] = send(term(lax.rem(x + 2, NX), di), ra.at[di], xdev(d))
        yield times[0]
        for d, di in ((1, 0), (-1, 1)):
            raw[d] = send(term(lax.rem(x + d + NX, NX), 1 - di), rr.at[di], xdev(d))
        yield times[1]
        for d, di in ((1, 0), (-1, 1)):
            first[d].wait_recv()
            accumulate(ra.at[di], term(lax.rem(x + d + NX, NX), di))
            second[d] = send(ra.at[di], rs.at[di], xdev(d))
        yield times[2]
        for d in (1, -1):
            raw[d].wait_recv()
            second[d].wait_recv()
        put(0, add3(term(x, 0), rs.at[0], rr.at[1]))
        put(1, add3(term(x, 1), rr.at[0], rs.at[1]))
        done.add(name)

    def add3(a, b, d):
        return (a[...].astype(f32) + b[...].astype(f32) + d[...].astype(f32)).astype(bf16)

    def term_z1(Z, h):
        return gin.at[2 * h : 2 * h + 2, 2:4, :, Z]

    for d, h in ((1, 0), (-1, 1), (1, 1), (-1, 0)):
        spawn(z_stream("z1", d, h, term_z1, rbz1, 0.5 + 2.8 * ((h == 0) != (d == 1)), 5.6), 0)

    def x_stage_one(yb):
        def term(X, h):
            return gin.at[X, yb, 2 * h : 2 * h + 2]

        def put(h, value):
            r1[yb, 2 * h : 2 * h + 2] = value

        t = 2.8 * yb
        return x_stream(("x1", yb), term, ra1.at[yb], rr1.at[yb], rs1.at[yb], put, (0.1 + yb / 100, 4.6 + t, 16.4 + t))

    for yb in range(2):
        spawn(x_stage_one(yb), 0)

    def z_stage_two(yb):
        yield 16.0
        yield from need(("x1", yb))
        t = clock["t"]

        def term(Z, h):
            return r1.at[h, :, Z]

        for d in (1, -1):
            spawn(z_stream("z2", d, yb, term, rbz2, t, 2.4), t)
        yield t + 0.1
        yield from need(("z2", 1, yb), ("z2", -1, yb))
        fin[yb] = add3(r1.at[yb, :, z], rbz2.at[0, yb, last(1, yb)], rbz2.at[1, yb, last(-1, yb)])
        done.add(("fin", yb))

    for yb in range(2):
        spawn(z_stage_two(yb), 1)

    def x_stage_two():
        yield 20.0
        for h in (0, 1):
            yield from need(("z1", 1, h), ("z1", -1, h))
            r2[2 * h : 2 * h + 2] = add3(
                gin.at[2 * h : 2 * h + 2, 2:4, :, z], rbz1.at[0, h, last(1, h)], rbz1.at[1, h, last(-1, h)]
            )

        def term(X, h):
            return r2.at[X, h]

        def put(h, value):
            fin[2 + h] = value

        t = clock["t"]
        yield from x_stream("x2", term, ra2, rr2, rs2, put, (t, t + 2.4, t + 4.8))

    spawn(x_stage_two(), 1)

    def left_roots():
        got = send(lroot.at[:, 1 - c], ly.at[y, c], sibling)
        yield 3.0
        load_l.wait()
        got.wait_recv()
        copies = {}
        for d in (1, -1):
            copies[d] = send(ly.at[y], ly.at[y], ydev(d))
        yield 12.0
        relays = []
        for d, oc in ((1, 0), (-1, 1)):
            copies[d].wait_recv()
            frm = lax.rem(y - d + NY, NY)
            relays.append(send(ly.at[frm, oc], ly.at[frm, oc], ydev(d)))
        yield 18.5
        for copy in relays:
            copy.wait_recv()
        for xb in range(NX):
            o, s = jnp.int32(0), jnp.int32(0)
            for yb in range(NY):
                o = o + jnp.where(y == yb, own[NY * xb + yb], 0)
                s = s + jnp.where(y == yb, place[NY * xb + yb], 0)
            lsel[xb] = ly[o // NC, lax.rem(o, NC), s]
        copies = []
        for k in range(1, NX):
            copies.append(send(lsel.at[lax.rem(x + k, NX)], lhome.at[x], xdev(k)))
        lhome[x] = lsel[x]
        yield 26.0
        for copy in copies:
            copy.wait_recv()
        lhs2[0 : NX * HALF] = lhome[...].reshape(NX * HALF, ORDER)
        done.add("left_roots")

    spawn(left_roots(), 0.6)

    def deliver(t, src, t0, hop):
        copies = []
        for k in range(1, NX):
            copies.append(send(src(lax.rem(x + k, NX)), held[t].at[y, x], xdev(k)))
        keep = local(src(x), held[t].at[y, x])
        yield t0 + hop
        keep.wait()
        for copy in copies:
            copy.wait_recv()
        copies = {}
        for d in (1, -1):
            copies[d] = send(held[t].at[y], held[t].at[y], ydev(d))
        yield t0 + 2.5 * hop
        relays = []
        for d, hb in ((1, 0), (-1, 1)):
            copies[d].wait_recv()
            frm = lax.rem(y - d + NY, NY)
            part = held[t].at[frm, 2 * hb : 2 * hb + 2]
            relays.append(send(part, part, ydev(d)))
        yield t0 + 3.5 * hop
        for copy in relays:
            copy.wait_recv()
        for s in range(SLOT_COUNT):
            b = theirs[s]
            stage[t, s] = held[t][lax.rem(b, NY), b // NY]
        got = send(stage.at[t], won.at[t, :, c], sibling)
        for s in range(SLOT_COUNT):
            b = mine[s]
            won[t, s, c] = held[t][lax.rem(b, NY), b // NY]
        yield t0 + 4 * hop
        got.wait_recv()
        done.add(("won", t))

    def used(s):
        return jnp.full((ROWS, ORDER), owned, jnp.int32) > s

    def row(s):
        return lax.broadcasted_iota(jnp.int32, (8, COLS), 0) == s

    def slot_rows(t, s):
        return won[t, s].reshape(ROWS, ORDER).astype(f32)

    norm_tile = {"v": jnp.zeros((8, COLS), f32)}
    stores = []

    def moments(t0):
        yield from need(("won", 0))
        load_1.wait()
        load_2.wait()
        for s in range(SLOT_COUNT):
            g = slot_rows(0, s)
            m1, m2 = m1v[s], m2v[s]
            n1 = jnp.where(used(s), beta_one * m1 + (1.0 - beta_one) * g, m1)
            n2 = jnp.where(used(s), beta_two * m2 + (1.0 - beta_two) * g * g, m2)
            out_1[s] = n1
            out_2[s] = n2
            adam = n1 / (jnp.sqrt(n2) + adam_eps)
            norm_tile["v"] = jnp.where(row(s), jnp.sum(adam * adam), norm_tile["v"])
        stores.append(local(out_1, first_out))
        stores.append(local(out_2, second_out))
        done.add("moments")

    def statistics(t, load, stat, out, dst):
        yield from need(("won", t))
        load.wait()
        for s in range(SLOT_COUNT):
            old = stat[s]
            out[s] = jnp.where(used(s), old + slot_rows(t, s) * (1.0 / ORDER), old)
        stores.append(local(out, dst))

    def vectors():
        copies = [send(vecg, vx.at[k - 1], xdev(k)) for k in range(1, NX)]
        yield 15.0
        for copy in copies:
            copy.wait_recv()
        vs[...] = vecg[...] + vx[0] + vx[1] + vx[2]
        yield 48.0
        yield from need("gathered")
        copies = [send(vs, vz.at[k - 1], zdev(k)) for k in range(1, NZ)]
        yield clock["t"] + 12.0
        total = vs[...]
        for k, copy in enumerate(copies):
            copy.wait_recv()
            total = total + vz[k]
        vec_out[...] = total

    spawn(vectors(), 0.7)

    def main():
        yield 22.0
        yield from need(("fin", 0), ("fin", 1), "x2")
        copies = []
        for k in range(1, N_MP):
            to = lax.rem(mp + k, N_MP)
            yt, ct = to // NC, lax.rem(to, NC)
            copies.append(
                send(
                    fin.at[yt, :, pl.ds(pl.multiple_of(ct * HALF, HALF), HALF)],
                    gfull.at[:, z, ct, :, pl.ds(pl.multiple_of(mp * COLS, COLS), COLS)],
                    (dp, to),
                )
            )
        keep = local(
            fin.at[y, :, pl.ds(pl.multiple_of(c * HALF, HALF), HALF)],
            gfull.at[:, z, c, :, pl.ds(pl.multiple_of(mp * COLS, COLS), COLS)],
        )
        t = clock["t"] + 3.5
        yield t
        keep.wait()
        for copy in copies:
            copy.wait_recv()

        over, ring = [], {}

        def chunk(h, src):
            return gfull.at[2 * h : 2 * h + 2, src, c]

        for h in (0, 1):
            for d in (1, -1):
                ring[d, h] = send(chunk(h, z), chunk(h, z), zdev(d))
        over.append(send(gfull.at[:, z, c], gfull.at[:, z, c], sibling))
        spawn(deliver(0, lambda xt: gfull.at[xt, z, c], t, 3.0), t)
        spawn(moments(t), t + 8)
        for s in range(4):
            for h in (0, 1):
                yield t + (s + 1) * 3.0 + h * 1.5
                for d in (1, -1):
                    if (d, h) not in ring:
                        continue
                    ring.pop((d, h)).wait_recv()
                    src = lax.rem(z - d * (s + 1) + NZ, NZ)
                    if s < 2 or (s == 2 and (h == 0) == (d == 1)):
                        ring[d, h] = send(chunk(h, src), chunk(h, src), zdev(d))
                    over.append(send(chunk(h, src), chunk(h, src), sibling))
        done.add("gathered")

        rows_of = NX * HALF
        i = lax.broadcasted_iota(jnp.int32, (rows_of, ORDER), 0)
        j = lax.broadcasted_iota(jnp.int32, (rows_of, ORDER), 1)
        wanted = (i // HALF) * (NZ * ROWS) + z * ROWS + c * HALF + lax.rem(i, HALF)
        lhs1[rows_of:] = jnp.where(j == wanted, 1.0, 0.0).astype(bf16)
        lhs1[0:rows_of] = gfull[:, z, c].reshape(rows_of, ORDER)
        for copy in over:
            copy.wait_recv()
        width = NZ * ROWS
        for n in range(NX):
            o = lax.dot_general(
                lhs1[...], gfull[n].reshape(width, ORDER), (((1,), (1,)), ((), ())), preferred_element_type=f32
            )
            res[1, :, :, n * width : (n + 1) * width] = o[0:rows_of].reshape(NX, HALF, width).astype(bf16)
            lhs2[rows_of:, n * width : (n + 1) * width] = o[rows_of:].astype(bf16)
        yield from need("left_roots")
        for n in range(NX):
            o = jnp.dot(
                lhs2[...],
                gfull[:, :, :, :, n * width : (n + 1) * width].reshape(ORDER, width),
                preferred_element_type=f32,
            )
            res[0, :, :, n * width : (n + 1) * width] = o[0:rows_of].reshape(NX, HALF, width).astype(bf16)
            res[2, :, :, n * width : (n + 1) * width] = o[rows_of:].reshape(NX, HALF, width).astype(bf16)
        t = clock["t"] + 3.0
        for r in range(3):
            spawn(deliver(1 + r, lambda xt, r=r: res.at[r, xt], t + 2.0 * r, 3.0), t + 0.01 * r)
        spawn(statistics(2, load_ls, lsv, out_l, left_out), t + 14)
        spawn(statistics(3, load_rs, rsv, out_r, right_out), t + 16)
        yield t + 10
        yield from need(("won", 1), "moments")
        load_r.wait()
        tile = norm_tile["v"]
        for s in range(SLOT_COUNT):
            p = jnp.dot(won[1, s].reshape(ROWS, ORDER), rrv[s], preferred_element_type=f32)
            prec[s] = p.astype(bf16)
            tile = jnp.where(row(SLOT_COUNT + s), jnp.sum(p * p), tile)
        norm_me[...] = tile
        copies_n = [send(norm_me, norm_z.at[k - 1], zdev(k)) for k in range(1, NZ)]
        copies_u = []
        for k in range(1, N_MP):
            to = lax.rem(mp + k, N_MP)
            cols = pl.ds(pl.multiple_of(to * COLS, COLS), COLS)
            copies_u.append(send(prec.at[:, :, cols], upd_in.at[mp], (dp, to)))
        keep = local(prec.at[:, :, pl.ds(pl.multiple_of(mp * COLS, COLS), COLS)], upd_in.at[mp])
        yield clock["t"] + 4.0
        for k, copy in enumerate(copies_n):
            copy.wait_recv()
            tile = tile + norm_z[k]
        norm_me2 = norm_x.at[NX - 1]
        norm_me2[...] = tile
        copies_n = [send(norm_me2, norm_x.at[k - 1], xdev(k)) for k in range(1, NX)]
        yield clock["t"] + 3.0
        for k, copy in enumerate(copies_n):
            copy.wait_recv()
            tile = tile + norm_x[k]
        cells = float(ORDER * ORDER)
        graft = jnp.sqrt(tile[0:SLOT_COUNT] / cells) / jnp.sqrt(tile[SLOT_COUNT:] / cells + graft_eps)
        norm_m[mp] = jnp.concatenate([graft, graft], axis=0)
        copies_n = [send(norm_m.at[mp], norm_m.at[mp], (dp, lax.rem(mp + k, N_MP))) for k in range(1, N_MP)]
        yield clock["t"] + 3.0
        keep.wait()
        for copy in copies_u + copies_n:
            copy.wait_recv()
        for b in range(BLOCKS):
            g = jnp.sum(jnp.where(row(place[b]), norm_m[own[b]], 0.0), axis=0, keepdims=True)
            upd_s[b] = (upd_in[own[b], place[b]].astype(f32) * g).astype(bf16)
        stores.append(local(upd_s, upd_out))

    spawn(main(), 2)
    run()
    for copy in stores:
        copy.wait()
    for copy in sent:
        copy.wait_send()
    assert counts["remote"] <= N_SEMS, counts


def body(
    grad_parts, owners, left_stat, right_stat, left_root, right_root, first_moment, second_moment,
    vec_grad, vec_first, vec_second,
):
    hbm = pl.BlockSpec(memory_space=pl.ANY)
    vmem = pl.BlockSpec(memory_space=pltpu.VMEM)
    smem = pl.BlockSpec(memory_space=pltpu.SMEM)
    slots = jax.ShapeDtypeStruct((SLOT_COUNT, ROWS, ORDER), f32)
    vec_rows = vec_grad.shape[1] // COLS
    V = pltpu.VMEM
    scratch = [
        V((NX, NY, NX, NZ, ROWS, COLS), bf16),
        V((2, 2, 4, 2, 2, NX, ROWS, COLS), bf16),
        V((2, 2, 4, NX, ROWS, COLS), bf16),
        V((2, 2, 2, NZ, ROWS, COLS), bf16),
        V((2, 2, 2, NZ, ROWS, COLS), bf16),
        V((2, 2, 2, NZ, ROWS, COLS), bf16),
        V((2, NX, ROWS, COLS), bf16),
        V((2, NX, ROWS, COLS), bf16),
        V((2, NX, ROWS, COLS), bf16),
        V((2, NX, NZ, ROWS, COLS), bf16),
        V((NX, 2, NX, ROWS, COLS), bf16),
        V((NY, NX, ROWS, COLS), bf16),
        V((NX, NZ, NC, HALF, ORDER), bf16),
        V((NY, NC, SLOT_COUNT, HALF, ORDER), bf16),
        V((NX, HALF, ORDER), bf16),
        V((NX, HALF, ORDER), bf16),
        V((2 * NX * HALF, ORDER), bf16),
        V((2 * NX * HALF, ORDER), bf16),
        V((3, NX, HALF, ORDER), bf16),
        *[V((NY, NX, HALF, ORDER), bf16)] * 4,
        V((4, SLOT_COUNT, HALF, ORDER), bf16),
        V((4, SLOT_COUNT, NC, HALF, ORDER), bf16),
        V((SLOT_COUNT, ORDER, ORDER), bf16),
        V((SLOT_COUNT, ROWS, ORDER), f32),
        V((SLOT_COUNT, ROWS, ORDER), f32),
        V((SLOT_COUNT, ROWS, ORDER), f32),
        V((SLOT_COUNT, ROWS, ORDER), f32),
        V((SLOT_COUNT, ROWS, ORDER), f32),
        V((SLOT_COUNT, ROWS, ORDER), f32),
        V((SLOT_COUNT, ROWS, ORDER), f32),
        V((SLOT_COUNT, ROWS, ORDER), f32),
        V((SLOT_COUNT, ROWS, ORDER), bf16),
        V((N_MP, SLOT_COUNT, ROWS, COLS), bf16),
        V((8, COLS), f32),
        V((NZ - 1, 8, COLS), f32),
        V((NX, 8, COLS), f32),
        V((N_MP, 8, COLS), f32),
        V((NX - 1, vec_rows, COLS), f32),
        V((vec_rows, COLS), f32),
        V((NZ - 1, vec_rows, COLS), f32),
        V((BLOCKS, ROWS, COLS), bf16),
        pltpu.SemaphoreType.DMA((N_SEMS,)),
        pltpu.SemaphoreType.DMA((N_SEMS,)),
        pltpu.SemaphoreType.DMA((24,)),
    ]
    block_update, left_new, right_new, first_new, second_new, vec_sum = pl.pallas_call(
        kernel,
        out_shape=(
            jax.ShapeDtypeStruct((BLOCKS, ROWS, COLS), bf16), slots, slots, slots, slots,
            jax.ShapeDtypeStruct((vec_rows, COLS), f32),
        ),
        in_specs=[smem] + [hbm] * 7 + [vmem],
        out_specs=(hbm,) * 5 + (vmem,),
        scratch_shapes=scratch,
        compiler_params=pltpu.CompilerParams(
            collective_id=0, has_side_effects=True, vmem_limit_bytes=62 * 1024 * 1024
        ),
    )(
        owners,
        grad_parts.reshape(NX, NY, NX, NZ, ROWS, COLS),
        left_root.reshape(SLOT_COUNT, NC, HALF, ORDER),
        right_root,
        left_stat,
        right_stat,
        first_moment,
        second_moment,
        vec_grad.astype(f32).reshape(vec_rows, COLS),
    )
    vec_sum = vec_sum.reshape(vec_first.shape)
    vec_first_new = beta_one * vec_first + (1.0 - beta_one) * vec_sum
    vec_second_new = beta_two * vec_second + (1.0 - beta_two) * vec_sum * vec_sum
    vec_update = (vec_first_new / (jnp.sqrt(vec_second_new) + adam_eps)).astype(bf16)
    return (
        block_update,
        left_new,
        right_new,
        first_new,
        second_new,
        vec_update,
        vec_first_new,
        vec_second_new,
    )


def solution(mesh):
    slots = P("mp", "dp", None)
    return jax.shard_map(
        body,
        mesh=mesh,
        in_specs=(
            P("dp", None, None, "mp"), P(), slots, slots, slots, P("mp", None, None), slots, slots,
            P("dp", "mp"), P("mp"), P("mp"),
        ),
        out_specs=(P(None, "dp", "mp"), slots, slots, slots, slots, P("mp"), P("mp"), P("mp")),
        check_vma=False,
    )
```

time: 519 us -> 120 us (0.23)
  waiting for transfers between devices: 315 us -> 0 us
  blocking collectives: 129 us -> 0 us
  Pallas kernels: 0 us -> 107 us
  starting transfers between devices: 32.9 us -> 0 us
  matrix products: 19.8 us -> 0 us
  between operations: 14.1 us -> 0.68 us
  local copies, waits for them, and re-layouts: 2.49 us -> 9.11 us
    reduce_scatter x1 -> x0, waiting for transfers between devices: 224 us -> none  [body(): lax.psum_scatter(grad_parts[0].astype(jnp.float32).astype(jnp.bfloat16),...]
    psum x1 -> x0, blocking collectives: 112 us -> none  [body(): lax.psum((square_adam, square_pre, vec_local), 'dp')]
    pallas_call x0 -> x1, Pallas kernels: none -> 107 us  [body(): pl.pallas_call(kernel, out_shape=(jax.ShapeDtypeStruct((BLOCKS, ROWS, COL...]
    all_gather x1 -> x0, waiting for transfers between devices: 90.5 us -> none  [body(): shard_rows = lax.all_gather(rounded_rows, 'dp', axis=1, tiled=True)]
    all_to_all x1 -> x0, starting transfers between devices: 32.8 us -> none  [body(): lax.all_to_all(update_rows.reshape(slot_count, row_count, owner_count, co...]
    dot_general x5 -> x0, matrix products: 19.8 us -> none  [the longest x1 8.86 us: body(): jnp.einsum('crk,ckm->crm', applied_acc.astype(jnp.bfloat16), right_root,...]
    all_to_all x1 -> x0, blocking collectives: 16.5 us -> none  [body(): lax.all_to_all(outgoing.astype(jnp.bfloat16), 'mp', split_axis=2, concat_...]
    unnamed x16 -> x9, local copies, waits for them, and re-layouts: 0.78 us -> 9.11 us
  transfers between devices with their start and end apart: 3 -> 0, of which waited for: 2 -> 0; matrix products, arithmetic and copies ran while one was open for 3% -> 0% of each run, Pallas kernels for 0% -> 0%
where the time goes in v2:
time: 120 us
  Pallas kernels  107 us (89%)
  local copies, waits for them, and re-layouts  9.11 us (8%)
  other arithmetic  2.85 us (2%)
    pallas_call x1, Pallas kernels, body(): pl.pallas_call(kernel, out_shape=(jax.ShapeDtypeStruct((BLOCKS, ROWS, COL...  107 us
    unnamed x9, local copies, waits for them, and re-layouts  9.11 us

profile of v2, /device:TPU:1, one launch (start us, length us, event | category | flops | bytes accessed | tf_op | source)
XLA Modules:
  0.0 119.5 jit_solution(8889468778751106671)
XLA Ops:
  0.6 0.0 copy-start
  0.6 0.0 copy-start.1
  0.7 1.4 %reshape.35 = f32[1,9216]{1,0:T(1,128)} convert(bf16[1,9216]{1,0:T(2,128)(2,1)} %param.19) | non-fusion elementwise | flops 9216 | bytes 55296 | tf_op jit(solution)/shard_map/reshape | solution.py:556
  2.1 106.9 %shard_map.170 = (bf16[16,32,128]{2,1,0:T(8,128)(2,1)}, f32[4,32,1024]{2,1,0:T(8,128)}, f32[4,32,1024]{2,1,0:T(8,128)}, f32[4,32,1024]{2,1,0:T(8,128)}, f32[4,32,1024]{2,1,0:T(8,128)}, /*index=5*/f32[72,128]{1,0:T(8,128)}) custom-call(s32[16]{0:T(128)} %owners.1, bf16[4,4,4,8,32,128]{5,4,3,2,1,0:T(8,128)(2,1)} %bitcast.10, ...), custom_call_target="tpu_custom_call" | custom-call | tf_op jit(solution)/shard_map/pallas_call | solution.py:535
  109.0 0.0 copy-done
  109.0 0.0 copy-done.1
  109.0 1.4 %divide_convert_fusion = (bf16[9216]{0:T(1024)(128)(2,1)}, f32[9216]{0:T(1024)}, f32[9216]{0:T(1024)}) fusion(f32[72,128]{1,0:T(8,128)} %get-tuple-element.19, f32[9216]{0:T(1024)S(1)} %copy-done, f32[9216]{0:T(1024)S(1)} %copy-done.1), kind=kLoop, calls=%fused_computation.4 | loop fusion | flops 92160 | bytes 202752 | tf_op jit(solution)/shard_map/convert_element_type | solution.py:561
  110.4 1.6 %copy.24 = bf16[16,32,128]{2,1,0:T(8,128)(2,1)} copy(bf16[16,32,128]{2,1,0:T(8,128)(2,1)} %get-tuple-element.31) | data formatting | bytes 262144
  112.0 1.9 %copy.25 = f32[4,32,1024]{2,1,0:T(8,128)} copy(f32[4,32,1024]{2,1,0:T(8,128)} %get-tuple-element.32) | data formatting | bytes 1048576
  113.9 1.9 %copy.26 = f32[4,32,1024]{2,1,0:T(8,128)} copy(f32[4,32,1024]{2,1,0:T(8,128)} %get-tuple-element.33) | data formatting | bytes 1048576
  115.8 1.9 %copy.27 = f32[4,32,1024]{2,1,0:T(8,128)} copy(f32[4,32,1024]{2,1,0:T(8,128)} %get-tuple-element.34) | data formatting | bytes 1048576
  117.6 1.9 %copy.28 = f32[4,32,1024]{2,1,0:T(8,128)} copy(f32[4,32,1024]{2,1,0:T(8,128)} %get-tuple-element.35) | data formatting | bytes 1048576
Async XLA Ops:
  0.6 108.4 %copy-start = (f32[9216]{0:T(1024)S(1)}, f32[9216]{0:T(1024)}, u32[]{:S(2)}) copy-start(f32[9216]{0:T(1024)} %param.21) | copy-start | bytes 110596
  0.6 108.4 %copy-start.1 = (f32[9216]{0:T(1024)S(1)}, f32[9216]{0:T(1024)}, u32[]{:S(2)}) copy-start(f32[9216]{0:T(1024)} %param.20) | copy-start | bytes 110596

commit v3 on v2

--- a/solution.py
+++ b/solution.py
@@ -476,6 +476,34 @@
     assert counts["remote"] <= N_SEMS, counts
 
 
+def finish(
+    upd, left, right, first, second, vec_sum, vec_first, vec_second,
+    upd_out, left_out, right_out, first_out, second_out, vec_out, vec_first_out, vec_second_out,
+    upd_v, slots_v, in_sems, out_sems,
+):
+    moves = []
+    for n, (src, dst) in enumerate(((left, left_out), (right, right_out), (first, first_out), (second, second_out))):
+        for s in range(SLOT_COUNT):
+            moves.append((src.at[s], slots_v.at[n, s], dst.at[s]))
+    moves.append((upd, upd_v, upd_out))
+    loads = [pltpu.make_async_copy(src, held, in_sems.at[i]) for i, (src, held, _) in enumerate(moves)]
+    for copy in loads:
+        copy.start()
+    total = vec_sum[...]
+    n1 = beta_one * vec_first[...] + (1.0 - beta_one) * total
+    n2 = beta_two * vec_second[...] + (1.0 - beta_two) * total * total
+    vec_first_out[...] = n1
+    vec_second_out[...] = n2
+    vec_out[...] = (n1 / (jnp.sqrt(n2) + adam_eps)).astype(bf16)
+    puts = []
+    for i, (_, held, dst) in enumerate(moves):
+        loads[i].wait()
+        puts.append(pltpu.make_async_copy(held, dst, out_sems.at[i]))
+        puts[i].start()
+    for copy in puts:
+        copy.wait()
+
+
 def body(
     grad_parts, owners, left_stat, right_stat, left_root, right_root, first_moment, second_moment,
     vec_grad, vec_first, vec_second,
@@ -555,19 +583,34 @@
         second_moment,
         vec_grad.astype(f32).reshape(vec_rows, COLS),
     )
-    vec_sum = vec_sum.reshape(vec_first.shape)
-    vec_first_new = beta_one * vec_first + (1.0 - beta_one) * vec_sum
-    vec_second_new = beta_two * vec_second + (1.0 - beta_two) * vec_sum * vec_sum
-    vec_update = (vec_first_new / (jnp.sqrt(vec_second_new) + adam_eps)).astype(bf16)
+    vec_f32 = jax.ShapeDtypeStruct((vec_rows, COLS), f32)
+    block_update, left_new, right_new, first_new, second_new, vec_update, vec_first_new, vec_second_new = pl.pallas_call(
+        finish,
+        out_shape=(
+            jax.ShapeDtypeStruct((BLOCKS, ROWS, COLS), bf16), slots, slots, slots, slots,
+            jax.ShapeDtypeStruct((vec_rows, COLS), bf16), vec_f32, vec_f32,
+        ),
+        in_specs=[hbm] * 5 + [vmem] * 3,
+        out_specs=(hbm,) * 5 + (vmem,) * 3,
+        scratch_shapes=[
+            V((BLOCKS, ROWS, COLS), bf16),
+            V((4, SLOT_COUNT, ROWS, ORDER), f32),
+            pltpu.SemaphoreType.DMA((4 * SLOT_COUNT + 1,)),
+            pltpu.SemaphoreType.DMA((4 * SLOT_COUNT + 1,)),
+        ],
+    )(
+        block_update, left_new, right_new, first_new, second_new, vec_sum,
+        vec_first.reshape(vec_rows, COLS), vec_second.reshape(vec_rows, COLS),
+    )
     return (
         block_update,
         left_new,
         right_new,
         first_new,
         second_new,
-        vec_update,
-        vec_first_new,
-        vec_second_new,
+        vec_update.reshape(vec_first.shape),
+        vec_first_new.reshape(vec_first.shape),
+        vec_second_new.reshape(vec_first.shape),
     )
 
 

time: 120 us -> 113 us (0.942)
  local copies, waits for them, and re-layouts: 9.11 us -> 0 us
  Pallas kernels: 107 us -> 111 us
  other arithmetic: 2.85 us -> 1.42 us
    unnamed x9 -> x0, local copies, waits for them, and re-layouts: 9.11 us -> none
    pallas_call x0 -> x1, Pallas kernels: none -> 4.07 us  [body(): pl.pallas_call(finish, out_shape=(jax.ShapeDtypeStruct((BLOCKS, ROWS, COL...]
    convert_element_type x1 -> x0, other arithmetic: 1.41 us -> none  [body(): (vec_first_new / (jnp.sqrt(vec_second_new) + adam_eps)).astype(bf16)]
where the time goes in v3:
time: 113 us
  Pallas kernels  111 us (98%)
  other arithmetic  1.42 us (1%)
    pallas_call x1, Pallas kernels, body(): pl.pallas_call(kernel, out_shape=(jax.ShapeDtypeStruct((BLOCKS, ROWS, COL...  107 us
    pallas_call x1, Pallas kernels, body(): pl.pallas_call(finish, out_shape=(jax.ShapeDtypeStruct((BLOCKS, ROWS, COL...  4.07 us

profile of v3, /device:TPU:1, one launch (start us, length us, event | category | flops | bytes accessed | tf_op | source)
XLA Modules:
  0.0 113.0 jit_solution(643728566665352129)
XLA Ops:
  0.6 1.4 %reshape.51 = f32[1,9216]{1,0:T(1,128)} convert(bf16[1,9216]{1,0:T(2,128)(2,1)} %param.19) | non-fusion elementwise | flops 9216 | bytes 55296 | tf_op jit(solution)/shard_map/reshape | solution.py:584
  2.1 106.9 %shard_map.170 = (bf16[16,32,128]{2,1,0:T(8,128)(2,1)}, f32[4,32,1024]{2,1,0:T(8,128)}, f32[4,32,1024]{2,1,0:T(8,128)}, f32[4,32,1024]{2,1,0:T(8,128)}, f32[4,32,1024]{2,1,0:T(8,128)}, /*index=5*/f32[72,128]{1,0:T(8,128)}) custom-call(s32[16]{0:T(128)} %owners.1, bf16[4,4,4,8,32,128]{5,4,3,2,1,0:T(8,128)(2,1)} %bitcast.8, bf16[4,2,16,1024]{3,2,1,0:T(8,128)(2,1)} %bitcast.9, ...), custom_call_target="tpu_custom_call" | custom-call | tf_op jit(solution)/shard_map/pallas_call | solution.py:563
  109.0 4.1 %shard_map.171 = (bf16[16,32,128]{2,1,0:T(8,128)(2,1)}, f32[4,32,1024]{2,1,0:T(8,128)}, f32[4,32,1024]{2,1,0:T(8,128)}, f32[4,32,1024]{2,1,0:T(8,128)}, f32[4,32...) custom-call(bf16[16,32,128]{2,1,0:T(8,128)(2,1)} %get-tuple-element.22.upd, ...), custom_call_target="tpu_custom_call" | custom-call | tf_op jit(solution)/shard_map/pallas_call | solution.py:587

commit v4 on v3

--- a/solution.py
+++ b/solution.py
@@ -17,7 +17,7 @@
 N_MP = NY * NC
 BLOCKS, SLOT_COUNT, ROWS, ORDER, COLS = 16, 4, 32, 1024, 128
 HALF = ROWS // NC
-N_SEMS = 224
+N_SEMS = 248
 bf16, f32 = jnp.bfloat16, jnp.float32
 
 
@@ -26,7 +26,7 @@
     upd_out, left_out, right_out, first_out, second_out, vec_out,
     gin, rbz1, rbz2, ra1, rr1, rs1, ra2, rr2, rs2, r1, r2, fin, gfull,
     ly, lsel, lhome, lhs1, lhs2, res, held0, held1, held2, held3, stage, won, rrv, lsv, rsv, m1v, m2v,
-    out_l, out_r, out_1, out_2, prec, upd_in, norm_me, norm_z, norm_x, norm_m, vx, vs, vz, upd_s,
+    out_l, out_r, out_1, out_2, prec, upd_in, norm_me, norm_z, norm_m, vx, vs, vz, upd_s,
     send_sems, recv_sems, local_sems,
 ):
     dp, mp = lax.axis_index("dp"), lax.axis_index("mp")
@@ -70,16 +70,10 @@
     load_l = local(lroot.at[:, c], ly.at[y, c])
 
     barrier = pltpu.get_barrier_semaphore()
-    partners = [xdev(k) for k in range(1, NX)] + [zdev(k) for k in range(1, NZ)]
+    partners = [(lax.rem(dp + k, NX * NZ), mp) for k in range(1, NX * NZ)]
     partners += [(dp, lax.rem(mp + k, N_MP)) for k in range(1, N_MP)]
     for device in partners:
         pl.semaphore_signal(barrier, inc=1, device_id=device, device_id_type=MESH)
-
-    load_r = local(rroot, rrv)
-    load_1 = local(mom1, m1v)
-    load_2 = local(mom2, m2v)
-    load_ls = local(lstat, lsv)
-    load_rs = local(rstat, rsv)
 
     own = [owners[b] for b in range(BLOCKS)]
     slot = []
@@ -104,8 +98,6 @@
     for b in range(BLOCKS):
         owned = owned + jnp.where(own[b] == mp, 1, 0)
 
-    load_z.wait()
-    load_x.wait()
     pl.semaphore_wait(barrier, len(partners))
 
     def accumulate(into, term):
@@ -133,10 +125,10 @@
         while not all(n in done for n in names):
             yield clock["t"] + 0.25
 
-    def z_stream(name, d, h, term, rb, t0, dt):
+    def z_stream(name, d, h, term, rb, t0, dt, origin=None):
         steps = 4 if (h == 0) == (d == 1) else 3
         di = 0 if d == 1 else 1
-        copy = send(term(lax.rem(z + d * steps + NZ, NZ), h), rb.at[di, h, 0], zdev(d))
+        copy = send((origin or term)(lax.rem(z + d * steps + NZ, NZ), h), rb.at[di, h, 0], zdev(d))
         for s in range(steps):
             yield t0 + (s + 1) * dt
             copy.wait_recv()
@@ -148,13 +140,13 @@
     def last(d, h):
         return 3 if (h == 0) == (d == 1) else 2
 
-    def x_stream(name, term, ra, rr, rs, put, times):
+    def x_stream(name, term, ra, rr, rs, put, times, origin=None):
         first, raw, second = {}, {}, {}
         for d, di in ((1, 0), (-1, 1)):
-            first[d] = send(term(lax.rem(x + 2, NX), di), ra.at[di], xdev(d))
+            first[d] = send((origin or term)(lax.rem(x + 2, NX), di), ra.at[di], xdev(d))
         yield times[0]
         for d, di in ((1, 0), (-1, 1)):
-            raw[d] = send(term(lax.rem(x + d + NX, NX), 1 - di), rr.at[di], xdev(d))
+            raw[d] = send((origin or term)(lax.rem(x + d + NX, NX), 1 - di), rr.at[di], xdev(d))
         yield times[1]
         for d, di in ((1, 0), (-1, 1)):
             first[d].wait_recv()
@@ -174,8 +166,11 @@
     def term_z1(Z, h):
         return gin.at[2 * h : 2 * h + 2, 2:4, :, Z]
 
+    def hbm_z1(Z, h):
+        return grad.at[2 * h : 2 * h + 2, 2:4, :, Z]
+
     for d, h in ((1, 0), (-1, 1), (1, 1), (-1, 0)):
-        spawn(z_stream("z1", d, h, term_z1, rbz1, 0.5 + 2.8 * ((h == 0) != (d == 1)), 5.6), 0)
+        spawn(z_stream("z1", d, h, term_z1, rbz1, 0.5 + 2.8 * ((h == 0) != (d == 1)), 5.6, hbm_z1), 0)
 
     def x_stage_one(yb):
         def term(X, h):
@@ -184,11 +179,29 @@
         def put(h, value):
             r1[yb, 2 * h : 2 * h + 2] = value
 
+        def origin(X, h):
+            return grad.at[X, yb, 2 * h : 2 * h + 2]
+
         t = 2.8 * yb
-        return x_stream(("x1", yb), term, ra1.at[yb], rr1.at[yb], rs1.at[yb], put, (0.1 + yb / 100, 4.6 + t, 16.4 + t))
+        times = (0.1 + yb / 100, 4.6 + t, 16.4 + t)
+        return x_stream(("x1", yb), term, ra1.at[yb], rr1.at[yb], rs1.at[yb], put, times, origin)
 
     for yb in range(2):
         spawn(x_stage_one(yb), 0)
+
+    later = {}
+
+    def loads():
+        load_x.wait()
+        load_z.wait()
+        later["1"] = local(mom1, m1v)
+        later["2"] = local(mom2, m2v)
+        later["ls"] = local(lstat, lsv)
+        later["rs"] = local(rstat, rsv)
+        later["r"] = local(rroot, rrv)
+        yield from ()
+
+    spawn(loads(), 2.0)
 
     def z_stage_two(yb):
         yield 16.0
@@ -309,8 +322,8 @@
 
     def moments(t0):
         yield from need(("won", 0))
-        load_1.wait()
-        load_2.wait()
+        later["1"].wait()
+        later["2"].wait()
         for s in range(SLOT_COUNT):
             g = slot_rows(0, s)
             m1, m2 = m1v[s], m2v[s]
@@ -326,7 +339,7 @@
 
     def statistics(t, load, stat, out, dst):
         yield from need(("won", t))
-        load.wait()
+        later[load].wait()
         for s in range(SLOT_COUNT):
             old = stat[s]
             out[s] = jnp.where(used(s), old + slot_rows(t, s) * (1.0 / ORDER), old)
@@ -425,18 +438,18 @@
         t = clock["t"] + 3.0
         for r in range(3):
             spawn(deliver(1 + r, lambda xt, r=r: res.at[r, xt], t + 2.0 * r, 3.0), t + 0.01 * r)
-        spawn(statistics(2, load_ls, lsv, out_l, left_out), t + 14)
-        spawn(statistics(3, load_rs, rsv, out_r, right_out), t + 16)
+        spawn(statistics(2, "ls", lsv, out_l, left_out), t + 14)
+        spawn(statistics(3, "rs", rsv, out_r, right_out), t + 16)
         yield t + 10
         yield from need(("won", 1), "moments")
-        load_r.wait()
+        later["r"].wait()
         tile = norm_tile["v"]
         for s in range(SLOT_COUNT):
             p = jnp.dot(won[1, s].reshape(ROWS, ORDER), rrv[s], preferred_element_type=f32)
             prec[s] = p.astype(bf16)
             tile = jnp.where(row(SLOT_COUNT + s), jnp.sum(p * p), tile)
         norm_me[...] = tile
-        copies_n = [send(norm_me, norm_z.at[k - 1], zdev(k)) for k in range(1, NZ)]
+        copies_n = [send(norm_me, norm_z.at[k - 1], (lax.rem(dp + k, NX * NZ), mp)) for k in range(1, NX * NZ)]
         copies_u = []
         for k in range(1, N_MP):
             to = lax.rem(mp + k, N_MP)
@@ -447,13 +460,6 @@
         for k, copy in enumerate(copies_n):
             copy.wait_recv()
             tile = tile + norm_z[k]
-        norm_me2 = norm_x.at[NX - 1]
-        norm_me2[...] = tile
-        copies_n = [send(norm_me2, norm_x.at[k - 1], xdev(k)) for k in range(1, NX)]
-        yield clock["t"] + 3.0
-        for k, copy in enumerate(copies_n):
-            copy.wait_recv()
-            tile = tile + norm_x[k]
         cells = float(ORDER * ORDER)
         graft = jnp.sqrt(tile[0:SLOT_COUNT] / cells) / jnp.sqrt(tile[SLOT_COUNT:] / cells + graft_eps)
         norm_m[mp] = jnp.concatenate([graft, graft], axis=0)
@@ -549,8 +555,7 @@
         V((SLOT_COUNT, ROWS, ORDER), bf16),
         V((N_MP, SLOT_COUNT, ROWS, COLS), bf16),
         V((8, COLS), f32),
-        V((NZ - 1, 8, COLS), f32),
-        V((NX, 8, COLS), f32),
+        V((NX * NZ - 1, 8, COLS), f32),
         V((N_MP, 8, COLS), f32),
         V((NX - 1, vec_rows, COLS), f32),
         V((vec_rows, COLS), f32),

time: 113 us -> 113 us (level)
  no operation moved by 1% of the time
where the time goes in v4:
time: 113 us
  Pallas kernels  111 us (98%)
  other arithmetic  1.42 us (1%)
    pallas_call x1, Pallas kernels, body(): pl.pallas_call(kernel, out_shape=(jax.ShapeDtypeStruct((BLOCKS, ROWS, COL...  107 us
    pallas_call x1, Pallas kernels, body(): pl.pallas_call(finish, out_shape=(jax.ShapeDtypeStruct((BLOCKS, ROWS, COL...  4.07 us

profile of v4, /device:TPU:1, one launch (start us, length us, event | category | flops | bytes accessed | tf_op | source)
XLA Modules:
  0.0 113.2 jit_solution(18061120214907052098)
XLA Ops:
  0.6 1.4 %reshape.51 = f32[1,9216]{1,0:T(1,128)} convert(bf16[1,9216]{1,0:T(2,128)(2,1)} %param.19) | non-fusion elementwise | flops 9216 | bytes 55296 | tf_op jit(solution)/shard_map/reshape | solution.py:589
  2.1 107.0 %shard_map.170 = (bf16[16,32,128]{2,1,0:T(8,128)(2,1)}, f32[4,32,1024]{2,1,0:T(8,128)}, f32[4,32,1024]{2,1,0:T(8,128)}, f32[4,32,1024]{2,1,0:T(8,128)}, f32[4,32,1024]{2,1,0:T(8,128)}, /*index=5*/f32[72,128]{1,0:T(8,128)}) custom-call(s32[16]{0:T(128)} %owners.1, bf16[4,4,4,8,32,128]{5,4,3,2,1,0:T(8,128)(2,1)} %bitcast.8, bf16[4,2,16,1024]{3,2,1,0:T(8,128)(2,1)} %bitcast.9, ...), custom_call_target="tpu_custom_call" | custom-call | tf_op jit(solution)/shard_map/pallas_call | solution.py:568
  109.1 4.1 %shard_map.171 = (bf16[16,32,128]{2,1,0:T(8,128)(2,1)}, f32[4,32,1024]{2,1,0:T(8,128)}, f32[4,32,1024]{2,1,0:T(8,128)}, f32[4,32,1024]{2,1,0:T(8,128)}, f32[4,32...) custom-call(bf16[16,32,128]{2,1,0:T(8,128)(2,1)} %get-tuple-element.22.upd, ...), custom_call_target="tpu_custom_call" | custom-call | tf_op jit(solution)/shard_map/pallas_call | solution.py:592
